TPU v7x, 32 devices: a whole 2x2x4 slice. The times are simulated.
32 devices in a mesh: mem: 4 (over z), tile: 8 (over y, x, core).
Axes of the slice: x: 2, y: 2, z: 4, core: 2. Of those that a mesh axis runs over, the one named last changes fastest.
Arguments:
- alpha: float32 [32, 8, 192, 384], P('mem', None, 'tile'), may hold values from -6 to 6
- ensemble: bfloat16 [2, 32, 8, 192, 384], P(None, 'mem', None, 'tile'), may hold values from -1 to 1
- innovation: float32 [2, 8, 192, 384], P(None, None, 'tile'), may hold values from -6 to 6
- precision: float32 [2, 8, 192, 384], P(None, None, 'tile'), may hold values from 0.5 to 8
- diffusivity: float32 [2, 8, 192, 384], P(None, None, 'tile'), may hold values from 0.01 to 0.48, as said below
Outputs:
- gradient: float32 [32, 8, 192, 384], P('mem', None, 'tile')
- increment: float32 [2, 8, 192, 384], P(None, None, 'tile')
Inputs may be any that keep to these rules, and one draw needn't show every extreme that they name: diffusivity[0] lies between 0.40 and 0.48 and diffusivity[1] between 0.01 and 0.02, so the four faces of a cell sum to at most 1.
All inputs are finite; a program needn't handle non-finite values.
Results may differ from a plain program's by a relative error of at most 0.0003.
Values sent between devices are 32-bit elements; how exact they have to be, the bound alone decides.
A program may use at most 64 MiB of HBM per device.

v0:
```python
import jax
import jax.numpy as jnp
from jax import lax
from jax.sharding import PartitionSpec as P

STEPS = 4


def extended(cells, sides, width):
    for axis, dim in sides:
        count = lax.axis_size(axis)
        head = lax.slice_in_dim(cells, 0, width, axis=dim)
        tail = lax.slice_in_dim(cells, cells.shape[dim] - width, cells.shape[dim], axis=dim)
        cells = jnp.concatenate(
            [
                lax.ppermute(tail, axis, [(i, (i + 1) % count) for i in range(count)]),
                cells,
                lax.ppermute(head, axis, [((i + 1) % count, i) for i in range(count)]),
            ],
            axis=dim,
        )
    return cells


def diffuse(field, coeffs, width):
    for sweep in range(width):
        columns = field.shape[2]
        zonal_face = coeffs[0, :, sweep : sweep + columns - 1]
        merid_face = coeffs[1, :, sweep + 1 : sweep + columns - 1]
        zonal_flux = zonal_face * (field[:, :, 1:] - field[:, :, :-1])
        interior = field[:, :, 1:-1]
        merid_flux = merid_face[:, :, :-1] * (interior[:, :, :, 1:] - interior[:, :, :, :-1])
        padding = jnp.zeros_like(interior[:, :, :, :1])
        north_flux = jnp.concatenate([merid_flux, padding], axis=3)
        south_flux = jnp.concatenate([padding, merid_flux], axis=3)
        field = interior + zonal_flux[:, :, 1:] - zonal_flux[:, :, :-1] + north_flux - south_flux
    return field


def per_device(alpha, ensemble, innovation, precision, diffusivity):
    coeffs = extended(diffusivity, (("tile", 2),), STEPS)
    padded = extended(alpha, (("tile", 2),), STEPS)
    localized = diffuse(padded, coeffs, STEPS)
    partial_sum = jnp.sum(ensemble.astype(jnp.float32) * localized[None], axis=1)
    increment = lax.psum(partial_sum, "mem")
    weighted = precision * (increment - innovation)
    projected = jnp.sum(ensemble.astype(jnp.float32) * weighted[:, None], axis=0)
    padded_adj = extended(projected, (("tile", 2),), STEPS)
    adjoint_field = diffuse(padded_adj, coeffs, STEPS)
    gradient = alpha + adjoint_field
    return (gradient, increment)


def solution(mesh):
    in_specs = (
        P("mem", None, "tile", None),
        P(None, "mem", None, "tile", None),
        P(None, None, "tile", None),
        P(None, None, "tile", None),
        P(None, None, "tile", None),
    )
    out_specs = (P("mem", None, "tile", None), P(None, None, "tile", None))
    return jax.shard_map(
        per_device, mesh=mesh, in_specs=in_specs, out_specs=out_specs, check_vma=False
    )
```

profile of v0, /device:TPU:1, one launch (start us, length us, event | category | flops | bytes accessed | tf_op | source)
XLA Modules:
  0.0 121.3 jit_solution(3033836365526358352)
XLA Ops:
  8.3 2.6 %collective-permute-start.2 = (f32[2,8,4,384]{3,2,1,0:T(4,128)S(1)}, f32[2,8,4,384]{3,2,1,0:T(4,128)S(1)}, u32[]{:S(2)}, u32[]{:S(2)}) collective-permute-start(f32[2,8,4,384]{3,2,1,0:T(4,128)S(1)} %get-tuple-element.8), channel_id=1, source_target_pairs={{0,1},{1,2},{2,3},{3,4},{4,5},{5,6},{6,7},{7,0},{8,9},{9,10},{10,1... | collective-permute-start | bytes 294920 | tf_op jit(solution)/shard_map/ppermute | solution.py:16
  11.0 1.5 %fusion.37 = (f32[8,8,4,384]{3,2,1,0:T(4,128)S(1)}, f32[8,8,4,384]{3,2,1,0:T(4,128)S(1)}) fusion(f32[8,8,24,384]{3,2,1,0:T(8,128)} %param.5), kind=kLoop, calls=%fused_computation.83 | loop fusion | bytes 1572864 | tf_op jit(solution)/shard_map/slice | solution.py:13
  12.5 1.8 %collective-permute-start = (f32[8,8,4,384]{3,1,2,0:T(8,128)S(1)}, f32[8,8,4,384]{3,1,2,0:T(8,128)S(1)}, u32[]{:S(2)}, u32[]{:S(2)}) collective-permute-start(f32[8,8,4,384]{3,1,2,0:T(8,128)S(1)} %copy.29), channel_id=1, source_target_pairs={{0,1},{1,2},{2,3},{3,4},{4,5},{5,6},{6,7},{7,0},{8,9},{9,10},{10,1... | collective-permute-start | bytes 1179656 | tf_op jit(solution)/shard_map/ppermute | solution.py:16
  18.6 2.6 %collective-permute-done = f32[8,8,4,384]{3,1,2,0:T(8,128)S(1)} collective-permute-done((f32[8,8,4,384]{3,1,2,0:T(8,128)S(1)}, f32[8,8,4,384]{3,1,2,0:T(8,128)S(1)}, u32[]{:S(2)}, u32[]{:S(2)}) %collective-permute-start) | collective-permute-done | bytes 393248 | tf_op jit(solution)/shard_map/ppermute | solution.py:16
  21.4 4.5 %collective-permute-done.1 = f32[8,8,4,384]{3,1,2,0:T(8,128)S(1)} collective-permute-done((f32[8,8,4,384]{3,1,2,0:T(8,128)S(1)}, f32[8,8,4,384]{3,1,2,0:T(8,128)S(1)}, u32[]{:S(2)}, u32[]{:S(2)}) %collective-permute-start.1) | collective-permute-done | bytes 393248 | tf_op jit(solution)/shard_map/ppermute | solution.py:18
  26.5 1.2 fusion.24
  28.2 1.7 %fusion.26 = f32[8,8,30,384]{3,2,1,0:T(8,128)S(1)} fusion(f32[8,8,31,384]{3,2,1,0:T(8,128)S(1)} %fusion.27, f32[8,8,32,384]{3,2,1,0:T(8,128)S(1)} %pad_maximum_fusion, f32[8,8,30,383]{3,2,1,0:T(8,128)S(1)} %fusion.24), kind=kLoop, calls=%fused_computation.52 | loop fusion | flops 2949120 | bytes 14737920 | tf_op jit(solution)/shard_map/sub | solution.py:36
  29.9 1.2 fusion.20
  31.7 1.7 %fusion.22 = f32[8,8,28,384]{3,2,1,0:T(8,128)S(1)} fusion(f32[8,8,29,384]{3,2,1,0:T(8,128)S(1)} %fusion.23, f32[8,8,30,384]{3,2,1,0:T(8,128)S(1)} %fusion.26, f32[8,8,28,383]{3,2,1,0:T(8,128)S(1)} %fusion.20), kind=kLoop, calls=%fused_computation.44 | loop fusion | flops 2752512 | bytes 13755392 | tf_op jit(solution)/shard_map/sub | solution.py:36
  33.4 1.2 fusion.16
  35.2 1.7 %fusion.18 = f32[8,8,26,384]{3,2,1,0:T(8,128)S(1)} fusion(f32[8,8,27,384]{3,2,1,0:T(8,128)S(1)} %fusion.19, f32[8,8,28,384]{3,2,1,0:T(8,128)S(1)} %fusion.22, f32[8,8,26,383]{3,2,1,0:T(8,128)S(1)} %fusion.16), kind=kLoop, calls=%fused_computation.36 | loop fusion | flops 2555904 | bytes 12772864 | tf_op jit(solution)/shard_map/sub | solution.py:36
  38.9 1.2 fusion.34
  40.6 1.3 %fusion = f32[2,8,24,384]{3,2,1,0:T(8,128)} fusion(bf16[2,8,8,24,384]{4,3,2,1,0:T(8,128)(2,1)S(1)} %copy-done.1, f32[8,8,24,384]{3,2,1,0:T(8,128)S(1)} %fusion.34), kind=kLoop, calls=%fused_computation.2 | loop fusion | flops 3391488 | bytes 5308416 | tf_op jit(solution)/shard_map/reduce_sum | solution.py:44
  41.9 39.6 %all-reduce.18.cloned.1.call-done = f32[2,8,24,384]{3,2,1,0:T(8,128)} async-done(((f32[2,8,24,384]{3,2,1,0:T(8,128)}), f32[2,8,24,384]{3,2,1,0:T(8,128)}) %all-reduce.18.cloned.1.call-update) | async-done | bytes 589840 | tf_op jit(solution)/shard_map/psum | solution.py:45
  81.5 1.6 %subtract_multiply_fusion = f32[2,8,24,384]{3,2,1,0:T(8,128)S(1)} fusion(f32[2,8,24,384]{3,2,1,0:T(8,128)} %param.8, f32[2,8,24,384]{3,2,1,0:T(8,128)} %all-reduce.18.cloned.1.call-done, f32[2,8,24,384]{3,2,1,0:T(8,128)} %param.7), kind=kLoop, calls=%fused_computation.72 | loop fusion | flops 294912 | bytes 2359296 | tf_op jit(solution)/shard_map/mul | solution.py:46
  84.4 2.4 %collective-permute-start.4 = (f32[8,8,4,384]{3,1,2,0:T(8,128)S(1)}, f32[8,8,4,384]{3,1,2,0:T(8,128)S(1)}, u32[]{:S(2)}, u32[]{:S(2)}) collective-permute-start(f32[8,8,4,384]{3,1,2,0:T(8,128)S(1)} %copy.25), channel_id=1, source_target_pairs={{0,1},{1,2},{2,3},{3,4},{4,5},{5,6},{6,7},{7,0},{8,9},{9,10},{10,1... | collective-permute-start | bytes 1179656 | tf_op jit(solution)/shard_map/ppermute | solution.py:16
  87.0 7.0 %collective-permute-done.4 = f32[8,8,4,384]{3,1,2,0:T(8,128)S(1)} collective-permute-done((f32[8,8,4,384]{3,1,2,0:T(8,128)S(1)}, f32[8,8,4,384]{3,1,2,0:T(8,128)S(1)}, u32[]{:S(2)}, u32[]{:S(2)}) %collective-permute-start.4) | collective-permute-done | bytes 393248 | tf_op jit(solution)/shard_map/ppermute | solution.py:16
  94.1 3.4 %collective-permute-done.5 = f32[8,8,4,384]{3,1,2,0:T(8,128)S(1)} collective-permute-done((f32[8,8,4,384]{3,1,2,0:T(8,128)S(1)}, f32[8,8,4,384]{3,1,2,0:T(8,128)S(1)}, u32[]{:S(2)}, u32[]{:S(2)}) %collective-permute-start.5) | collective-permute-done | bytes 393248 | tf_op jit(solution)/shard_map/ppermute | solution.py:18
  100.2 1.7 %fusion.13 = f32[8,8,30,384]{3,2,1,0:T(8,128)S(1)} fusion(f32[8,8,31,384]{3,2,1,0:T(8,128)S(1)} %fusion.14, f32[8,8,32,384]{3,2,1,0:T(8,128)S(1)} %pad_maximum_fusion.1, f32[8,8,30,383]{3,2,1,0:T(8,128)S(1)} %fusion.11), kind=kLoop, calls=%fused_computation.26 | loop fusion | flops 2949120 | bytes 14737920 | tf_op jit(solution)/shard_map/sub | solution.py:36
  102.0 1.2 fusion.7
  103.7 1.7 %fusion.9 = f32[8,8,28,384]{3,2,1,0:T(8,128)S(1)} fusion(f32[8,8,29,384]{3,2,1,0:T(8,128)S(1)} %fusion.10, f32[8,8,30,384]{3,2,1,0:T(8,128)S(1)} %fusion.13, f32[8,8,28,383]{3,2,1,0:T(8,128)S(1)} %fusion.7), kind=kLoop, calls=%fused_computation.18 | loop fusion | flops 2752512 | bytes 13755392 | tf_op jit(solution)/shard_map/sub | solution.py:36
  105.4 1.2 fusion.3
  107.2 1.7 %fusion.5 = f32[8,8,26,384]{3,2,1,0:T(8,128)S(1)} fusion(f32[8,8,27,384]{3,2,1,0:T(8,128)S(1)} %fusion.6, f32[8,8,28,384]{3,2,1,0:T(8,128)S(1)} %fusion.9, f32[8,8,26,383]{3,2,1,0:T(8,128)S(1)} %fusion.3), kind=kLoop, calls=%fused_computation.10 | loop fusion | flops 2555904 | bytes 12772864 | tf_op jit(solution)/shard_map/sub | solution.py:36
  110.8 2.9 %fusion.31 = f32[8,8,24,384]{3,2,1,0:T(8,128)} fusion(f32[8,8,24,384]{3,2,1,0:T(8,128)S(1)} %copy-done, f32[8,8,25,384]{3,2,1,0:T(8,128)S(1)} %fusion.2, f32[8,8,26,384]{3,2,1,0:T(8,128)S(1)} %fusion.5, f32[8,8,24,383]{3,2,1,0:T(8,128)S(1)} %fusion.28), kind=kLoop, calls=%fused_computation.63 | loop fusion | flops 2949120 | bytes 14149632 | tf_op jit(solution)/shard_map/add | solution.py:50
  (75 shorter events, 18.2 us)
Async XLA Ops:
  7.2 7.3 %copy-start.3 = (f32[2,8,24,384]{3,2,1,0:T(8,128)S(1)}, f32[2,8,24,384]{3,2,1,0:T(8,128)}, u32[]{:S(2)}) copy-start(f32[2,8,24,384]{3,2,1,0:T(8,128)} %param.9) | copy-start | bytes 1769476
  7.2 74.3 %all-reduce.18.cloned.1.call-start = ((), (), s32[]{:S(2)}) async-start(), calls=%async_computation | async-start | bytes 1179648 | tf_op jit(solution)/shard_map/psum | solution.py:45
  8.3 6.9 %collective-permute-start.2 = (f32[2,8,4,384]{3,2,1,0:T(4,128)S(1)}, f32[2,8,4,384]{3,2,1,0:T(4,128)S(1)}, u32[]{:S(2)}, u32[]{:S(2)}) collective-permute-start(f32[2,8,4,384]{3,2,1,0:T(4,128)S(1)} %get-tuple-element.8), channel_id=1, source_target_pairs={{0,1},{1,2},{2,3},{3,4},{4,5},{5,6},{6,7},{7,0},{8,9},{9,10},{10,1... | collective-permute-start | bytes 294920 | tf_op jit(solution)/shard_map/ppermute | solution.py:16
  11.0 4.3 %collective-permute-start.3 = (f32[2,8,4,384]{3,2,1,0:T(4,128)S(1)}, f32[2,8,4,384]{3,2,1,0:T(4,128)S(1)}, u32[]{:S(2)}, u32[]{:S(2)}) collective-permute-start(f32[2,8,4,384]{3,2,1,0:T(4,128)S(1)} %get-tuple-element.9), channel_id=1, source_target_pairs={{1,0},{2,1},{3,2},{4,3},{5,4},{6,5},{7,6},{0,7},{9,8},{10,9},{11,1... | collective-permute-start | bytes 294920 | tf_op jit(solution)/shard_map/ppermute | solution.py:18
  12.5 8.7 %collective-permute-start = (f32[8,8,4,384]{3,1,2,0:T(8,128)S(1)}, f32[8,8,4,384]{3,1,2,0:T(8,128)S(1)}, u32[]{:S(2)}, u32[]{:S(2)}) collective-permute-start(f32[8,8,4,384]{3,1,2,0:T(8,128)S(1)} %copy.29), channel_id=1, source_target_pairs={{0,1},{1,2},{2,3},{3,4},{4,5},{5,6},{6,7},{7,0},{8,9},{9,10},{10,1... | collective-permute-start | bytes 1179656 | tf_op jit(solution)/shard_map/ppermute | solution.py:16
  14.4 11.5 %collective-permute-start.1 = (f32[8,8,4,384]{3,1,2,0:T(8,128)S(1)}, f32[8,8,4,384]{3,1,2,0:T(8,128)S(1)}, u32[]{:S(2)}, u32[]{:S(2)}) collective-permute-start(f32[8,8,4,384]{3,1,2,0:T(8,128)S(1)} %copy.30), channel_id=1, source_target_pairs={{1,0},{2,1},{3,2},{4,3},{5,4},{6,5},{7,6},{0,7},{9,8},{10,9},{11,1... | collective-permute-start | bytes 1179656 | tf_op jit(solution)/shard_map/ppermute | solution.py:18
  15.4 11.1 %copy-start.12 = (f32[8,30,384]{2,1,0:T(8,128)}, f32[8,30,384]{2,1,0:T(8,128)S(1)}, u32[]{:S(2)}) copy-start(f32[8,30,384]{2,1,0:T(8,128)S(1)} %slice_bitcast_fusion.4) | copy-start | bytes 1105924
  15.4 10.5 %copy-start = (f32[8,8,24,384]{3,2,1,0:T(8,128)S(1)}, f32[8,8,24,384]{3,2,1,0:T(8,128)}, u32[]{:S(2)}) copy-start(f32[8,8,24,384]{3,2,1,0:T(8,128)} %param.5) | copy-start | bytes 7077892
  15.5 12.2 %copy-start.10 = (f32[8,31,384]{2,1,0:T(8,128)}, f32[8,31,384]{2,1,0:T(8,128)S(1)}, u32[]{:S(2)}) copy-start(f32[8,31,384]{2,1,0:T(8,128)S(1)} %slice_bitcast_fusion.5) | copy-start | bytes 1142788
  28.2 1.7 %copy-start.9 = (f32[8,28,384]{2,1,0:T(8,128)S(1)}, f32[8,28,384]{2,1,0:T(8,128)}, u32[]{:S(2)}) copy-start(f32[8,28,384]{2,1,0:T(8,128)} %slice_bitcast_fusion.2) | copy-start | bytes 1032196
  29.9 1.2 copy-start.7
  31.7 1.7 %copy-start.4 = (f32[8,26,384]{2,1,0:T(8,128)S(1)}, f32[8,26,384]{2,1,0:T(8,128)}, u32[]{:S(2)}) copy-start(f32[8,26,384]{2,1,0:T(8,128)} %slice_bitcast_fusion) | copy-start | bytes 958468
  33.4 1.2 copy-start.5
  36.9 1.0 copy-start.14
  38.9 1.7 %copy-start.1 = (bf16[2,8,8,24,384]{4,3,2,1,0:T(8,128)(2,1)S(1)}, bf16[2,8,8,24,384]{4,3,2,1,0:T(8,128)(2,1)}, u32[]{:S(2)}) copy-start(bf16[2,8,8,24,384]{4,3,2,1,0:T(8,128)(2,1)} %param.6) | copy-start | bytes 7077892
  81.5 2.2 %copy-start.2 = (bf16[2,8,8,24,384]{4,3,2,1,0:T(8,128)(2,1)S(1)}, bf16[2,8,8,24,384]{4,3,2,1,0:T(8,128)(2,1)}, u32[]{:S(2)}) copy-start(bf16[2,8,8,24,384]{4,3,2,1,0:T(8,128)(2,1)} %param.6) | copy-start | bytes 7077892
  84.4 9.5 %collective-permute-start.4 = (f32[8,8,4,384]{3,1,2,0:T(8,128)S(1)}, f32[8,8,4,384]{3,1,2,0:T(8,128)S(1)}, u32[]{:S(2)}, u32[]{:S(2)}) collective-permute-start(f32[8,8,4,384]{3,1,2,0:T(8,128)S(1)} %copy.25), channel_id=1, source_target_pairs={{0,1},{1,2},{2,3},{3,4},{4,5},{5,6},{6,7},{7,0},{8,9},{9,10},{10,1... | collective-permute-start | bytes 1179656 | tf_op jit(solution)/shard_map/ppermute | solution.py:16
  86.9 10.5 %collective-permute-start.5 = (f32[8,8,4,384]{3,1,2,0:T(8,128)S(1)}, f32[8,8,4,384]{3,1,2,0:T(8,128)S(1)}, u32[]{:S(2)}, u32[]{:S(2)}) collective-permute-start(f32[8,8,4,384]{3,1,2,0:T(8,128)S(1)} %copy.26), channel_id=1, source_target_pairs={{1,0},{2,1},{3,2},{4,3},{5,4},{6,5},{7,6},{0,7},{9,8},{10,9},{11,1... | collective-permute-start | bytes 1179656 | tf_op jit(solution)/shard_map/ppermute | solution.py:18
  97.5 1.0 copy-start.13
  98.5 1.2 copy-start.11
  102.0 1.2 copy-start.8
  105.4 1.2 copy-start.6
  108.9 1.0 copy-start.15
  110.8 2.9 %copy-start.16 = (f32[2,8,24,384]{3,2,1,0:T(8,128)S(1)}, f32[2,8,24,384]{3,2,1,0:T(8,128)}, u32[]{:S(2)}) copy-start(f32[2,8,24,384]{3,2,1,0:T(8,128)} %all-reduce.18.cloned.1.call-done) | copy-start | bytes 1769476
Sparse Core Ops, SparseCore 0:
  42.1 39.3 all-reduce.17
where the time goes:
time: 122 us; the launch traced here: 121 us
  waiting for transfers between devices  57 us (47%)
  other arithmetic  32.3 us (26%)
  between operations  14.5 us (12%)
  local copies, waits for them, and re-layouts  10.5 us (9%)
  starting transfers between devices  7.02 us (6%)
    psum x1, waiting for transfers between devices, per_device(): increment = lax.psum(partial_sum, 'mem')  39.6 us
    sub x7, other arithmetic, diffuse(): interior + zonal_flux[:, :, 1:] - zonal_flux[:, :, :-1] + north_flux  11.5 us
    ppermute x3, waiting for transfers between devices, extended(): lax.ppermute(tail, axis, [(i, (i + 1) % count) for i in range(count)])  9.61 us
    mul x8, other arithmetic, diffuse(): merid_face[:, :, :-1] * (interior[:, :, :, 1:] - interior[:, :, :, :-1])  9.07 us
    ppermute x3, waiting for transfers between devices, extended(): lax.ppermute(head, axis, [((i + 1) % count, i) for i in range(count)])  7.86 us
    ppermute x3, starting transfers between devices, extended(): lax.ppermute(tail, axis, [(i, (i + 1) % count) for i in range(count)])  6.86 us
    mul x9, other arithmetic, diffuse(): zonal_flux = zonal_face * (field[:, :, 1:] - field[:, :, :-1])  4.23 us
    unnamed x37, local copies, waits for them, and re-layouts  3.27 us
  transfers between devices with their start and end apart: 7, of which 5 were waited for; matrix products, arithmetic and copies ran while one was open for 5% of the time, Pallas kernels for 0%

commit v1 on v0

--- a/solution.py
+++ b/solution.py
@@ -42,7 +42,11 @@
     padded = extended(alpha, (("tile", 2),), STEPS)
     localized = diffuse(padded, coeffs, STEPS)
     partial_sum = jnp.sum(ensemble.astype(jnp.float32) * localized[None], axis=1)
-    increment = lax.psum(partial_sum, "mem")
+    increment = partial_sum
+    for hop in (1, 2):
+        increment = increment + lax.ppermute(
+            increment, "mem", [(dev, dev ^ hop) for dev in range(4)]
+        )
     weighted = precision * (increment - innovation)
     projected = jnp.sum(ensemble.astype(jnp.float32) * weighted[:, None], axis=0)
     padded_adj = extended(projected, (("tile", 2),), STEPS)

time: 122 us -> 112 us (0.918)
  the two profiles are of different devices: /device:TPU:1 before, /device:TPU:0 now
where the time goes in v1:
time: 112 us
  waiting for transfers between devices  54.7 us (49%)
  other arithmetic  33.1 us (30%)
  starting transfers between devices  15.2 us (14%)
  local copies, waits for them, and re-layouts  7.58 us (7%)
    ppermute x2, waiting for transfers between devices, per_device(): lax.ppermute(increment, 'mem', [(dev, dev ^ hop) for dev in range(4)])  40 us
    ppermute x3, waiting for transfers between devices, extended(): lax.ppermute(tail, axis, [(i, (i + 1) % count) for i in range(count)])  14.7 us
    sub x7, other arithmetic, diffuse(): interior + zonal_flux[:, :, 1:] - zonal_flux[:, :, :-1] + north_flux  11.4 us
    mul x8, other arithmetic, diffuse(): merid_face[:, :, :-1] * (interior[:, :, :, 1:] - interior[:, :, :, :-1])  11.1 us
    ppermute x3, starting transfers between devices, extended(): lax.ppermute(head, axis, [((i + 1) % count, i) for i in range(count)])  8.29 us
    ppermute x2, starting transfers between devices, per_device(): lax.ppermute(increment, 'mem', [(dev, dev ^ hop) for dev in range(4)])  6.2 us
    mul x9, other arithmetic, diffuse(): zonal_flux = zonal_face * (field[:, :, 1:] - field[:, :, :-1])  4.24 us
    add x1, other arithmetic, per_device(): gradient = alpha + adjoint_field  2.88 us
  transfers between devices with their start and end apart: 8, of which 4 were waited for; matrix products, arithmetic and copies ran while one was open for 4% of the time, Pallas kernels for 0%

profile of v1, /device:TPU:0, one launch (start us, length us, event | category | flops | bytes accessed | tf_op | source)
XLA Modules:
  0.0 111.6 jit_solution(4236631067475827801)
XLA Ops:
  2.3 2.9 %collective-permute-start.3 = (f32[2,8,4,384]{3,2,1,0:T(4,128)S(1)}, f32[2,8,4,384]{3,2,1,0:T(4,128)S(1)}, u32[]{:S(2)}, u32[]{:S(2)}) collective-permute-start(f32[2,8,4,384]{3,2,1,0:T(4,128)S(1)} %get-tuple-element.11), channel_id=1, source_target_pairs={{1,0},{2,1},{3,2},{4,3},{5,4},{6,5},{7,6},{0,7},{9,8},{10,9},{11,1... | collective-permute-start | bytes 294920 | tf_op jit(solution)/shard_map/ppermute | solution.py:18
  5.2 1.5 %fusion.37 = (f32[8,8,4,384]{3,2,1,0:T(4,128)S(1)}, f32[8,8,4,384]{3,2,1,0:T(4,128)S(1)}) fusion(f32[8,8,24,384]{3,2,1,0:T(8,128)} %param.5), kind=kLoop, calls=%fused_computation.83 | loop fusion | bytes 1572864 | tf_op jit(solution)/shard_map/slice | solution.py:13
  6.9 2.7 %collective-permute-start.1 = (f32[8,8,4,384]{3,1,2,0:T(8,128)S(1)}, f32[8,8,4,384]{3,1,2,0:T(8,128)S(1)}, u32[]{:S(2)}, u32[]{:S(2)}) collective-permute-start(f32[8,8,4,384]{3,1,2,0:T(8,128)S(1)} %copy.30), channel_id=1, source_target_pairs={{1,0},{2,1},{3,2},{4,3},{5,4},{6,5},{7,6},{0,7},{9,8},{10,9},{11,1... | collective-permute-start | bytes 1179656 | tf_op jit(solution)/shard_map/ppermute | solution.py:18
  12.2 5.2 %collective-permute-done = f32[8,8,4,384]{3,1,2,0:T(8,128)S(1)} collective-permute-done((f32[8,8,4,384]{3,1,2,0:T(8,128)S(1)}, f32[8,8,4,384]{3,1,2,0:T(8,128)S(1)}, u32[]{:S(2)}, u32[]{:S(2)}) %collective-permute-start) | collective-permute-done | bytes 393248 | tf_op jit(solution)/shard_map/ppermute | solution.py:16
  18.2 1.2 %fusion.24 = f32[8,8,30,383]{3,2,1,0:T(8,128)S(1)} fusion(f32[8,8,32,384]{3,2,1,0:T(8,128)S(1)} %pad_maximum_fusion, f32[8,30,383]{2,1,0:T(8,128)S(1)} %bitcast.24), kind=kLoop, calls=%fused_computation.49 | loop fusion | flops 1470720 | bytes 9192000 | tf_op jit(solution)/shard_map/mul | solution.py:32
  19.9 1.7 %fusion.26 = f32[8,8,30,384]{3,2,1,0:T(8,128)S(1)} fusion(f32[8,8,31,384]{3,2,1,0:T(8,128)S(1)} %fusion.27, f32[8,8,32,384]{3,2,1,0:T(8,128)S(1)} %pad_maximum_fusion, f32[8,8,30,383]{3,2,1,0:T(8,128)S(1)} %fusion.24), kind=kLoop, calls=%fused_computation.52 | loop fusion | flops 2949120 | bytes 14737920 | tf_op jit(solution)/shard_map/sub | solution.py:36
  21.7 2.2 %fusion.20 = f32[8,8,28,383]{3,2,1,0:T(8,128)S(1)} fusion(f32[8,8,30,384]{3,2,1,0:T(8,128)S(1)} %fusion.26, f32[8,28,383]{2,1,0:T(8,128)} %bitcast.22), kind=kLoop, calls=%fused_computation.41 | loop fusion | flops 1372672 | bytes 8579200 | tf_op jit(solution)/shard_map/mul | solution.py:32
  24.4 1.7 %fusion.22 = f32[8,8,28,384]{3,2,1,0:T(8,128)S(1)} fusion(f32[8,8,29,384]{3,2,1,0:T(8,128)S(1)} %fusion.23, f32[8,8,30,384]{3,2,1,0:T(8,128)S(1)} %fusion.26, f32[8,8,28,383]{3,2,1,0:T(8,128)S(1)} %fusion.20), kind=kLoop, calls=%fused_computation.44 | loop fusion | flops 2752512 | bytes 13755392 | tf_op jit(solution)/shard_map/sub | solution.py:36
  26.1 1.2 %fusion.16 = f32[8,8,26,383]{3,2,1,0:T(8,128)S(1)} fusion(f32[8,8,28,384]{3,2,1,0:T(8,128)S(1)} %fusion.22, f32[8,26,383]{2,1,0:T(8,128)S(1)} %bitcast.20), kind=kLoop, calls=%fused_computation.33 | loop fusion | flops 1274624 | bytes 7966400 | tf_op jit(solution)/shard_map/mul | solution.py:32
  27.9 1.7 %fusion.18 = f32[8,8,26,384]{3,2,1,0:T(8,128)S(1)} fusion(f32[8,8,27,384]{3,2,1,0:T(8,128)S(1)} %fusion.19, f32[8,8,28,384]{3,2,1,0:T(8,128)S(1)} %fusion.22, f32[8,8,26,383]{3,2,1,0:T(8,128)S(1)} %fusion.16), kind=kLoop, calls=%fused_computation.36 | loop fusion | flops 2555904 | bytes 12772864 | tf_op jit(solution)/shard_map/sub | solution.py:36
  31.7 1.2 %fusion.34 = f32[8,8,24,384]{3,2,1,0:T(8,128)S(1)} fusion(f32[8,8,25,384]{3,2,1,0:T(8,128)S(1)} %fusion.15, f32[8,8,26,384]{3,2,1,0:T(8,128)S(1)} %fusion.18, f32[8,8,24,383]{3,2,1,0:T(8,128)S(1)} %fusion.32), kind=kLoop, calls=%fused_computation.69 | loop fusion | flops 2359296 | bytes 11790336 | tf_op jit(solution)/shard_map/sub | solution.py:36
  33.9 3.0 %collective-permute-start.4 = (f32[2,8,24,384]{3,2,1,0:T(8,128)S(1)}, f32[2,8,24,384]{3,2,1,0:T(8,128)S(1)}, u32[]{:S(2)}, u32[]{:S(2)}) collective-permute-start(f32[2,8,24,384]{3,2,1,0:T(8,128)S(1)} %fusion), channel_id=1, source_target_pairs={{0,8},{8,0},{16,24},{24,16},{1,9},{9,1},{17,25},{25,17},{2,10},{10... | collective-permute-start | bytes 1769480 | tf_op jit(solution)/shard_map/ppermute | solution.py:47
  36.9 13.9 %collective-permute-done.4 = f32[2,8,24,384]{3,2,1,0:T(8,128)S(1)} collective-permute-done((f32[2,8,24,384]{3,2,1,0:T(8,128)S(1)}, f32[2,8,24,384]{3,2,1,0:T(8,128)S(1)}, u32[]{:S(2)}, u32[]{:S(2)}) %collective-permute-start.4) | collective-permute-done | bytes 589856 | tf_op jit(solution)/shard_map/ppermute | solution.py:47
  50.9 3.2 %collective-permute-start.5 = (f32[2,8,24,384]{3,2,1,0:T(8,128)S(1)}, f32[2,8,24,384]{3,2,1,0:T(8,128)S(1)}, u32[]{:S(2)}, u32[]{:S(2)}) collective-permute-start(f32[2,8,24,384]{3,2,1,0:T(8,128)S(1)} %add.97), channel_id=1, source_target_pairs={{0,16},{8,24},{16,0},{24,8},{1,17},{9,25},{17,1},{25,9},{2,18},{10... | collective-permute-start | bytes 1769480 | tf_op jit(solution)/shard_map/ppermute | solution.py:47
  54.1 26.1 %collective-permute-done.5 = f32[2,8,24,384]{3,2,1,0:T(8,128)S(1)} collective-permute-done((f32[2,8,24,384]{3,2,1,0:T(8,128)S(1)}, f32[2,8,24,384]{3,2,1,0:T(8,128)S(1)}, u32[]{:S(2)}, u32[]{:S(2)}) %collective-permute-start.5) | collective-permute-done | bytes 589856 | tf_op jit(solution)/shard_map/ppermute | solution.py:47
  82.0 2.7 %collective-permute-start.7 = (f32[8,8,4,384]{3,1,2,0:T(8,128)S(1)}, f32[8,8,4,384]{3,1,2,0:T(8,128)S(1)}, u32[]{:S(2)}, u32[]{:S(2)}) collective-permute-start(f32[8,8,4,384]{3,1,2,0:T(8,128)S(1)} %copy.26), channel_id=1, source_target_pairs={{1,0},{2,1},{3,2},{4,3},{5,4},{6,5},{7,6},{0,7},{9,8},{10,9},{11,1... | collective-permute-start | bytes 1179656 | tf_op jit(solution)/shard_map/ppermute | solution.py:18
  84.7 9.5 %collective-permute-done.6 = f32[8,8,4,384]{3,1,2,0:T(8,128)S(1)} collective-permute-done((f32[8,8,4,384]{3,1,2,0:T(8,128)S(1)}, f32[8,8,4,384]{3,1,2,0:T(8,128)S(1)}, u32[]{:S(2)}, u32[]{:S(2)}) %collective-permute-start.6) | collective-permute-done | bytes 393248 | tf_op jit(solution)/shard_map/ppermute | solution.py:16
  95.4 1.2 %fusion.11 = f32[8,8,30,383]{3,2,1,0:T(8,128)S(1)} fusion(f32[8,8,32,384]{3,2,1,0:T(8,128)S(1)} %pad_maximum_fusion.1, f32[8,30,383]{2,1,0:T(8,128)S(1)} %bitcast.25), kind=kLoop, calls=%fused_computation.23 | loop fusion | flops 1470720 | bytes 9192000 | tf_op jit(solution)/shard_map/mul | solution.py:32
  97.2 1.7 %fusion.13 = f32[8,8,30,384]{3,2,1,0:T(8,128)S(1)} fusion(f32[8,8,31,384]{3,2,1,0:T(8,128)S(1)} %fusion.14, f32[8,8,32,384]{3,2,1,0:T(8,128)S(1)} %pad_maximum_fusion.1, f32[8,8,30,383]{3,2,1,0:T(8,128)S(1)} %fusion.11), kind=kLoop, calls=%fused_computation.26 | loop fusion | flops 2949120 | bytes 14737920 | tf_op jit(solution)/shard_map/sub | solution.py:36
  98.9 2.2 %fusion.7 = f32[8,8,28,383]{3,2,1,0:T(8,128)S(1)} fusion(f32[8,8,30,384]{3,2,1,0:T(8,128)S(1)} %fusion.13, f32[8,28,383]{2,1,0:T(8,128)} %bitcast.23), kind=kLoop, calls=%fused_computation.15 | loop fusion | flops 1372672 | bytes 8579200 | tf_op jit(solution)/shard_map/mul | solution.py:32
  101.6 1.7 %fusion.9 = f32[8,8,28,384]{3,2,1,0:T(8,128)S(1)} fusion(f32[8,8,29,384]{3,2,1,0:T(8,128)S(1)} %fusion.10, f32[8,8,30,384]{3,2,1,0:T(8,128)S(1)} %fusion.13, f32[8,8,28,383]{3,2,1,0:T(8,128)S(1)} %fusion.7), kind=kLoop, calls=%fused_computation.18 | loop fusion | flops 2752512 | bytes 13755392 | tf_op jit(solution)/shard_map/sub | solution.py:36
  103.4 1.2 %fusion.3 = f32[8,8,26,383]{3,2,1,0:T(8,128)S(1)} fusion(f32[8,8,28,384]{3,2,1,0:T(8,128)S(1)} %fusion.9, f32[8,26,383]{2,1,0:T(8,128)S(1)} %bitcast.21), kind=kLoop, calls=%fused_computation.7 | loop fusion | flops 1274624 | bytes 7966400 | tf_op jit(solution)/shard_map/mul | solution.py:32
  105.1 1.7 %fusion.5 = f32[8,8,26,384]{3,2,1,0:T(8,128)S(1)} fusion(f32[8,8,27,384]{3,2,1,0:T(8,128)S(1)} %fusion.6, f32[8,8,28,384]{3,2,1,0:T(8,128)S(1)} %fusion.9, f32[8,8,26,383]{3,2,1,0:T(8,128)S(1)} %fusion.3), kind=kLoop, calls=%fused_computation.10 | loop fusion | flops 2555904 | bytes 12772864 | tf_op jit(solution)/shard_map/sub | solution.py:36
  108.7 2.9 %fusion.31 = f32[8,8,24,384]{3,2,1,0:T(8,128)} fusion(f32[8,8,24,384]{3,2,1,0:T(8,128)S(1)} %copy-done, f32[8,8,25,384]{3,2,1,0:T(8,128)S(1)} %fusion.2, f32[8,8,26,384]{3,2,1,0:T(8,128)S(1)} %fusion.5, f32[8,8,24,383]{3,2,1,0:T(8,128)S(1)} %fusion.28), kind=kLoop, calls=%fused_computation.63 | loop fusion | flops 2949120 | bytes 14149632 | tf_op jit(solution)/shard_map/add | solution.py:54
  (68 shorter events, 16.3 us)
Async XLA Ops:
  0.6 9.0 %copy-start.2 = (f32[2,8,24,384]{3,2,1,0:T(8,128)S(1)}, f32[2,8,24,384]{3,2,1,0:T(8,128)}, u32[]{:S(2)}) copy-start(f32[2,8,24,384]{3,2,1,0:T(8,128)} %param.9) | copy-start | bytes 1769476
  1.8 8.6 %collective-permute-start.2 = (f32[2,8,4,384]{3,2,1,0:T(4,128)S(1)}, f32[2,8,4,384]{3,2,1,0:T(4,128)S(1)}, u32[]{:S(2)}, u32[]{:S(2)}) collective-permute-start(f32[2,8,4,384]{3,2,1,0:T(4,128)S(1)} %get-tuple-element.10), channel_id=1, source_target_pairs={{0,1},{1,2},{2,3},{3,4},{4,5},{5,6},{6,7},{7,0},{8,9},{9,10},{10,1... | collective-permute-start | bytes 294920 | tf_op jit(solution)/shard_map/ppermute | solution.py:16
  2.3 8.0 %collective-permute-start.3 = (f32[2,8,4,384]{3,2,1,0:T(4,128)S(1)}, f32[2,8,4,384]{3,2,1,0:T(4,128)S(1)}, u32[]{:S(2)}, u32[]{:S(2)}) collective-permute-start(f32[2,8,4,384]{3,2,1,0:T(4,128)S(1)} %get-tuple-element.11), channel_id=1, source_target_pairs={{1,0},{2,1},{3,2},{4,3},{5,4},{6,5},{7,6},{0,7},{9,8},{10,9},{11,1... | collective-permute-start | bytes 294920 | tf_op jit(solution)/shard_map/ppermute | solution.py:18
  6.8 10.6 %collective-permute-start = (f32[8,8,4,384]{3,1,2,0:T(8,128)S(1)}, f32[8,8,4,384]{3,1,2,0:T(8,128)S(1)}, u32[]{:S(2)}, u32[]{:S(2)}) collective-permute-start(f32[8,8,4,384]{3,1,2,0:T(8,128)S(1)} %copy.29), channel_id=1, source_target_pairs={{0,1},{1,2},{2,3},{3,4},{4,5},{5,6},{6,7},{7,0},{8,9},{9,10},{10,1... | collective-permute-start | bytes 1179656 | tf_op jit(solution)/shard_map/ppermute | solution.py:16
  6.9 10.7 %collective-permute-start.1 = (f32[8,8,4,384]{3,1,2,0:T(8,128)S(1)}, f32[8,8,4,384]{3,1,2,0:T(8,128)S(1)}, u32[]{:S(2)}, u32[]{:S(2)}) collective-permute-start(f32[8,8,4,384]{3,1,2,0:T(8,128)S(1)} %copy.30), channel_id=1, source_target_pairs={{1,0},{2,1},{3,2},{4,3},{5,4},{6,5},{7,6},{0,7},{9,8},{10,9},{11,1... | collective-permute-start | bytes 1179656 | tf_op jit(solution)/shard_map/ppermute | solution.py:18
  10.5 7.7 %copy-start.7 = (f32[8,30,384]{2,1,0:T(8,128)}, f32[8,30,384]{2,1,0:T(8,128)S(1)}, u32[]{:S(2)}) copy-start(f32[8,30,384]{2,1,0:T(8,128)S(1)} %slice_bitcast_fusion.4) | copy-start | bytes 1105924
  10.5 7.2 %copy-start = (f32[8,8,24,384]{3,2,1,0:T(8,128)S(1)}, f32[8,8,24,384]{3,2,1,0:T(8,128)}, u32[]{:S(2)}) copy-start(f32[8,8,24,384]{3,2,1,0:T(8,128)} %param.5) | copy-start | bytes 7077892
  10.5 8.9 %copy-start.5 = (f32[8,31,384]{2,1,0:T(8,128)}, f32[8,31,384]{2,1,0:T(8,128)S(1)}, u32[]{:S(2)}) copy-start(f32[8,31,384]{2,1,0:T(8,128)S(1)} %slice_bitcast_fusion.5) | copy-start | bytes 1142788
  21.6 2.2 %copy-start.3 = (f32[8,29,384]{2,1,0:T(8,128)S(1)}, f32[8,29,384]{2,1,0:T(8,128)}, u32[]{:S(2)}) copy-start(f32[8,29,384]{2,1,0:T(8,128)} %slice_bitcast_fusion.3) | copy-start | bytes 1069060
  29.6 1.0 copy-start.9
  31.7 1.7 %copy-start.1 = (bf16[2,8,8,24,384]{4,3,2,1,0:T(8,128)(2,1)S(1)}, bf16[2,8,8,24,384]{4,3,2,1,0:T(8,128)(2,1)}, u32[]{:S(2)}) copy-start(bf16[2,8,8,24,384]{4,3,2,1,0:T(8,128)(2,1)} %param.6) | copy-start | bytes 7077892
  33.3 46.9 %copy-start.11 = (f32[2,8,24,384]{3,2,1,0:T(8,128)S(1)}, f32[2,8,24,384]{3,2,1,0:T(8,128)}, u32[]{:S(2)}) copy-start(f32[2,8,24,384]{3,2,1,0:T(8,128)} %param.8) | copy-start | bytes 1769476
  33.3 46.9 %copy-start.12 = (f32[2,8,24,384]{3,2,1,0:T(8,128)S(1)}, f32[2,8,24,384]{3,2,1,0:T(8,128)}, u32[]{:S(2)}) copy-start(f32[2,8,24,384]{3,2,1,0:T(8,128)} %param.7) | copy-start | bytes 1769476
  33.9 16.9 %collective-permute-start.4 = (f32[2,8,24,384]{3,2,1,0:T(8,128)S(1)}, f32[2,8,24,384]{3,2,1,0:T(8,128)S(1)}, u32[]{:S(2)}, u32[]{:S(2)}) collective-permute-start(f32[2,8,24,384]{3,2,1,0:T(8,128)S(1)} %fusion), channel_id=1, source_target_pairs={{0,8},{8,0},{16,24},{24,16},{1,9},{9,1},{17,25},{25,17},{2,10},{10... | collective-permute-start | bytes 1769480 | tf_op jit(solution)/shard_map/ppermute | solution.py:47
  50.9 29.2 %collective-permute-start.5 = (f32[2,8,24,384]{3,2,1,0:T(8,128)S(1)}, f32[2,8,24,384]{3,2,1,0:T(8,128)S(1)}, u32[]{:S(2)}, u32[]{:S(2)}) collective-permute-start(f32[2,8,24,384]{3,2,1,0:T(8,128)S(1)} %add.97), channel_id=1, source_target_pairs={{0,16},{8,24},{16,0},{24,8},{1,17},{9,25},{17,1},{25,9},{2,18},{10... | collective-permute-start | bytes 1769480 | tf_op jit(solution)/shard_map/ppermute | solution.py:47
  81.9 12.3 %collective-permute-start.6 = (f32[8,8,4,384]{3,1,2,0:T(8,128)S(1)}, f32[8,8,4,384]{3,1,2,0:T(8,128)S(1)}, u32[]{:S(2)}, u32[]{:S(2)}) collective-permute-start(f32[8,8,4,384]{3,1,2,0:T(8,128)S(1)} %copy.25), channel_id=1, source_target_pairs={{0,1},{1,2},{2,3},{3,4},{4,5},{5,6},{6,7},{7,0},{8,9},{9,10},{10,1... | collective-permute-start | bytes 1179656 | tf_op jit(solution)/shard_map/ppermute | solution.py:16
  82.0 12.3 %collective-permute-start.7 = (f32[8,8,4,384]{3,1,2,0:T(8,128)S(1)}, f32[8,8,4,384]{3,1,2,0:T(8,128)S(1)}, u32[]{:S(2)}, u32[]{:S(2)}) collective-permute-start(f32[8,8,4,384]{3,1,2,0:T(8,128)S(1)} %copy.26), channel_id=1, source_target_pairs={{1,0},{2,1},{3,2},{4,3},{5,4},{6,5},{7,6},{0,7},{9,8},{10,9},{11,1... | collective-permute-start | bytes 1179656 | tf_op jit(solution)/shard_map/ppermute | solution.py:18
  94.4 1.0 copy-start.8
  95.4 1.2 %copy-start.6 = (f32[8,31,384]{2,1,0:T(8,128)S(1)}, f32[8,31,384]{2,1,0:T(8,128)}, u32[]{:S(2)}) copy-start(f32[8,31,384]{2,1,0:T(8,128)} %copy-done.5) | copy-start | bytes 1142788
  98.9 2.2 %copy-start.4 = (f32[8,29,384]{2,1,0:T(8,128)S(1)}, f32[8,29,384]{2,1,0:T(8,128)}, u32[]{:S(2)}) copy-start(f32[8,29,384]{2,1,0:T(8,128)} %slice_bitcast_fusion.3) | copy-start | bytes 1069060
  106.8 1.0 copy-start.10
